TPU v7x, 32 devices: a whole 2x2x4 slice. The times are simulated.
32 devices in a mesh: grp: 4 (over y, core), tbl: 8 (over z, x).
Axes of the slice: x: 2, y: 2, z: 4, core: 2. Of those that a mesh axis runs over, the one named last changes fastest.
Arguments:
- user_feats: bfloat16 [512, 128], P(('grp', 'tbl')), may hold values from -6 to 6
- tower_in: bfloat16 [128, 4096], replicated, may hold values from -0.5 to 0.5
- tower_out: bfloat16 [4096, 256], replicated, may hold values from -0.09375 to 0.09375
- table: bfloat16 [2048, 256], P('tbl'), may hold values from -3 to 3
- inter_weight: bfloat16 [256, 512], replicated, may hold values from -0.375 to 0.375
- out_weight: float32 [512], replicated, may hold values from -0.3 to 0.3
- ids: int32 [32, 8, 4, 32], P(('grp', 'tbl')), may hold values from 0 to 255
- live: int32 [32, 8], P(('grp', 'tbl')), may hold values from 1 to 32, as said below
- req_of: int32 [32, 8, 32], P(('grp', 'tbl')), may hold values from 0 to 127
- labels: float32 [32, 8, 32], P(('grp', 'tbl')), may hold values from 0 to 1
Outputs:
- scores: float32 [32, 8, 32], P(('grp', 'tbl'))
- grad_tower_in: float32 [128, 4096], replicated
- grad_tower_out: float32 [4096, 256], replicated
- grad_inter: float32 [256, 512], replicated
- grad_out: float32 [512], replicated
- grad_table: float32 [2048, 256], P('tbl')
Inputs may be any that keep to these rules, and one draw needn't show every extreme that they name: In every draw, in each group, some device gets 32 live slots from every owner; the others get between 1 and 32 live slots from each owner.
All inputs are finite; a program needn't handle non-finite values.
Results may differ from a plain program's by a relative error of at most 0.0067.
Values may be sent and summed in bfloat16 or wider, within the bound.
A program may use at most 64 MiB of HBM per device.

v0:
```python
import math

import jax
import jax.numpy as jnp
from jax import lax
from jax.sharding import PartitionSpec as P


def silu_slope(value):
    sig = jax.nn.sigmoid(value)
    return sig * (1.0 + value * (1.0 - sig))


def body(
    user_feats, tower_in, tower_out, table, inter_weight, out_weight, ids, live, req_of, labels
):
    highest = lax.Precision.HIGHEST
    groups = lax.axis_size("grp")
    shards = lax.axis_size("tbl")
    width = table.shape[1]
    slots = ids.shape[3]
    rows_table = table.shape[0]
    pre = jnp.dot(user_feats, tower_in, preferred_element_type=jnp.float32)
    hidden = jax.nn.silu(pre).astype(jnp.bfloat16)
    users = jnp.dot(hidden, tower_out, preferred_element_type=jnp.float32).astype(jnp.bfloat16)
    everyone = lax.all_gather(users, "tbl", axis=0, tiled=True)
    local_ids = ids[0]
    summed = jnp.sum(table[local_ids].astype(jnp.float32), axis=1)
    pooled = summed.astype(jnp.bfloat16)
    received = lax.all_to_all(pooled, "tbl", split_axis=0, concat_axis=0, tiled=True)
    items = received.reshape(-1, width)
    request = req_of[0].reshape(-1)
    chosen = everyone[request]
    cross = (items.astype(jnp.float32) * chosen.astype(jnp.float32)).astype(jnp.bfloat16)
    inner = jnp.dot(cross, inter_weight, preferred_element_type=jnp.float32)
    act = jax.nn.silu(inner)
    score = jnp.sum(act * out_weight, axis=1)
    factor = 1.0 / math.sqrt(groups * shards * shards * slots)
    slot_index = jnp.arange(slots, dtype=jnp.int32)
    mask = (slot_index[None, :] < live[0][:, None]).reshape(-1)
    target = labels[0].reshape(-1)
    grad_score = jnp.where(mask, jax.nn.sigmoid(score) - target, 0.0) * factor
    dinner = (grad_score[:, None] * out_weight * silu_slope(inner)).astype(jnp.bfloat16)
    grad_inter = jnp.einsum("ce,ch->eh", cross, dinner, preferred_element_type=jnp.float32)
    grad_out = jnp.sum(grad_score[:, None] * act, axis=0)
    dcross = jnp.einsum("ch,eh->ce", dinner, inter_weight, preferred_element_type=jnp.float32)
    d_item = dcross * chosen.astype(jnp.float32)
    d_user = dcross * items.astype(jnp.float32)
    user_terms = jax.ops.segment_sum(d_user, request, num_segments=everyone.shape[0])
    d_users = lax.psum_scatter(user_terms, "tbl", scatter_dimension=0, tiled=True)
    returned = lax.all_to_all(
        d_item.reshape(shards, slots, width), "tbl", split_axis=0, concat_axis=0, tiled=True
    )
    flat_back = returned.reshape(-1, width)
    table_local = jnp.zeros((rows_table, width), jnp.float32)
    for bag in range(local_ids.shape[1]):
        table_local = table_local + jax.ops.segment_sum(
            flat_back, local_ids[:, bag, :].reshape(-1), num_segments=rows_table
        )
    grad_tower_out = jnp.dot(hidden.astype(jnp.float32).T, d_users, precision=highest)
    d_hidden = jnp.dot(d_users, tower_out.astype(jnp.float32).T, precision=highest)
    d_pre = d_hidden * silu_slope(pre)
    grad_tower_in = jnp.dot(user_feats.astype(jnp.float32).T, d_pre, precision=highest)
    totals = lax.psum((grad_tower_in, grad_tower_out, grad_inter, grad_out), ("grp", "tbl"))
    grad_table = lax.psum(table_local, "grp")
    scores = score.reshape(1, shards, slots)
    return (scores, totals[0], totals[1], totals[2], totals[3], grad_table)


def solution(mesh):
    placed = (
        P(("grp", "tbl"), None),
        P(),
        P(),
        P("tbl", None),
        P(),
        P(),
        P(("grp", "tbl"), None, None, None),
        P(("grp", "tbl"), None),
        P(("grp", "tbl"), None, None),
        P(("grp", "tbl"), None, None),
    )
    return jax.shard_map(
        body,
        mesh=mesh,
        in_specs=placed,
        out_specs=(P(("grp", "tbl"), None, None), P(), P(), P(), P(), P("tbl", None)),
        check_vma=False,
    )
```

profile of v0, /device:TPU:0, one launch (start us, length us, event | category | flops | bytes accessed | tf_op | source)
XLA Modules:
  0.0 343.9 jit_solution(7475186172980140353)
XLA Ops:
  7.2 0.9 compare_select_fusion
  8.2 4.4 %gather_fusion = bf16[1024,256]{1,0:T(8,128)(2,1)S(1)} fusion(bf16[256,256]{1,0:T(8,128)(2,1)} %param.13, s32[1024]{0:T(1024)S(1)} %broadcast_clamp_fusion), kind=kCustom, calls=%fused_computation | custom fusion | bytes 1052672 | tf_op jit(solution)/shard_map/gather | solution.py:28
  12.6 0.7 reduce_sum.30
  13.3 7.4 %all-to-all-start = ((bf16[8,32,256]{2,1,0:T(8,128)(2,1)}), bf16[8,32,256]{2,1,0:T(8,128)(2,1)S(1)}, u32[]{:S(2)}, u32[]{:S(2)}) async-start(bf16[8,32,256]{2,1,0:T(8,128)(2,1)} %reduce_sum.30), calls=%async_computation | async-start | bytes 262144 | tf_op jit(solution)/shard_map/all_to_all | solution.py:30
  20.9 1.5 fusion.11
  22.4 0.4 convolution_convert_fusion
  23.1 31.0 %all_gather.3 = bf16[128,256]{1,0:T(8,128)(2,1)S(1)} all-gather(bf16[16,256]{1,0:T(8,128)(2,1)S(1)} %convolution_convert_fusion), channel_id=1, replica_groups=mesh['grp'=4,'tbl'=8] {'tbl'}, dimensions={0}, use_global_device_ids=true | all-gather | bytes 73728 | tf_op jit(solution)/shard_map/all_gather | solution.py:26
  54.1 1.2 gather_fusion.1
  55.3 0.4 multiply_reduce_fusion.1
  55.8 0.3 multiply_reduce_fusion
  56.0 1.0 convert_multiply_fusion.2
  57.0 2.6 scatter_custom_fusion
  59.7 1.0 fusion.12
  60.7 62.4 %reduce-scatter.2.cloned.1.call-done = f32[16,256]{1,0:T(8,128)} async-done(((f32[128,256]{1,0:T(8,128)}), f32[16,256]{1,0:T(8,128)}) %reduce-scatter.2.cloned.1.call-update) | async-done | bytes 16400 | tf_op jit(solution)/shard_map/reduce_scatter | solution.py:50
  123.2 2.5 convolution_multiply_fusion
  125.7 3.1 convolution_bitcast_fusion
  128.8 3.9 %fusion.10 = f32[4096,256]{1,0:T(8,128)} fusion(f32[16,256]{1,0:T(8,128)S(1)} %copy-done.4, f32[16,4096]{1,0:T(8,128)S(1)} %fusion.11), kind=kOutput, calls=%fused_computation.40 | convolution fusion | flops 201654272 | bytes 4472832 | tf_op jit(solution)/shard_map/dot_general | solution.py:60
  132.7 3.6 %all-to-all-start.1 = ((f32[8,32,256]{2,1,0:T(8,128)}), f32[8,32,256]{2,1,0:T(8,128)S(1)}, u32[]{:S(2)}, u32[]{:S(2)}) async-start(f32[8,32,256]{2,1,0:T(8,128)} %bitcast.8), calls=%async_computation.2 | async-start | bytes 524288 | tf_op jit(solution)/shard_map/all_to_all | solution.py:51
  136.8 11.1 %all-to-all-done.1 = f32[8,32,256]{2,1,0:T(8,128)S(1)} async-done(((f32[8,32,256]{2,1,0:T(8,128)}), f32[8,32,256]{2,1,0:T(8,128)S(1)}, u32[]{:S(2)}, u32[]{:S(2)}) %all-to-all-start.1) | async-done | bytes 262176 | tf_op jit(solution)/shard_map/all_to_all | solution.py:51
  147.8 2.2 scatter_custom_fusion.1
  150.0 2.0 scatter_custom_fusion.2
  152.1 2.0 scatter_custom_fusion.4
  154.1 2.1 scatter_fusion
  156.2 0.7 add.89
  157.0 0.7 reshape.108
  157.6 39.4 %psum.38 = f32[512]{0:T(512)} all-reduce(f32[512]{0:T(512)S(1)} %get-tuple-element.25), channel_id=1, replica_groups=mesh['grp'=4,'tbl'=8] {'grp','tbl'}, use_global_device_ids=true, to_apply=%region_8.9 | all-reduce | flops 512 | bytes 4096 | tf_op jit(solution)/shard_map/psum | solution.py:64
  197.0 99.0 %all-reduce.6.cloned.1.call-done = (f32[128,4096]{0,1:T(8,128)}, f32[4096,256]{1,0:T(8,128)}, f32[256,512]{1,0:T(8,128)}) async-done(((f32[128,4096]{0,1:T(8,128)}, f32[4096,256]{1,0:T(8,128)}, f32[256,512]{1,0:T(8,128)}), (f32[128,4096]{0,1:T(8,128)}, f32[4096,256]{1,0:T(8,128)}, f32[256,512]{1,0:T(8,128)})) %all-reduce.6.cloned.1.call-update) | async-done | bytes 6815760 | tf_op jit(solution)/shard_map/psum | solution.py:64
  296.0 2.9 copy.17
  298.9 32.4 %all-reduce.4.cloned.1.call-done = f32[256,256]{1,0:T(8,128)} async-done(((f32[256,256]{1,0:T(8,128)}), f32[256,256]{1,0:T(8,128)}) %all-reduce.4.cloned.1.call-update) | async-done | bytes 262160 | tf_op jit(solution)/shard_map/psum | solution.py:65
  331.3 4.5 %copy.23 = f32[4096,256]{1,0:T(8,128)} copy(f32[4096,256]{1,0:T(8,128)} %get-tuple-element.33) | data formatting | bytes 8388608
  335.9 0.8 copy.24
  336.7 0.7 copy.25
  (46 shorter events, 1.2 us)
Async XLA Ops:
  7.2 15.2 %copy-start = (bf16[4096,256]{1,0:T(8,128)(2,1)S(1)}, bf16[4096,256]{1,0:T(8,128)(2,1)}, u32[]{:S(2)}) copy-start(bf16[4096,256]{1,0:T(8,128)(2,1)} %param.12) | copy-start | bytes 6291460
  8.1 12.6 %copy-start.7 = (s32[1,8,32]{2,1,0:T(8,128)S(1)}, s32[1,8,32]{2,1,0:T(8,128)}, u32[]{:S(2)}) copy-start(s32[1,8,32]{2,1,0:T(8,128)} %param.18) | copy-start | bytes 3076
  8.1 12.7 %copy-start.6 = (bf16[16,128]{1,0:T(8,128)(2,1)S(1)}, bf16[16,128]{1,0:T(8,128)(2,1)}, u32[]{:S(2)}) copy-start(bf16[16,128]{1,0:T(8,128)(2,1)} %param.10) | copy-start | bytes 12292
  13.3 9.4 %copy-start.10 = (s32[1,8]{1,0:T(1,128)S(1)}, s32[1,8]{1,0:T(1,128)}, u32[]{:S(2)}) copy-start(s32[1,8]{1,0:T(1,128)} %param.17) | copy-start | bytes 100
  13.3 9.7 %copy-start.8 = (f32[1,8,32]{2,1,0:T(8,128)S(1)}, f32[1,8,32]{2,1,0:T(8,128)}, u32[]{:S(2)}) copy-start(f32[1,8,32]{2,1,0:T(8,128)} %param.19) | copy-start | bytes 3076
  13.3 42.0 %all-to-all-start = ((bf16[8,32,256]{2,1,0:T(8,128)(2,1)}), bf16[8,32,256]{2,1,0:T(8,128)(2,1)S(1)}, u32[]{:S(2)}, u32[]{:S(2)}) async-start(bf16[8,32,256]{2,1,0:T(8,128)(2,1)} %reduce_sum.30), calls=%async_computation | async-start | bytes 262144 | tf_op jit(solution)/shard_map/all_to_all | solution.py:30
  20.7 102.4 %reduce-scatter.2.cloned.1.call-start = ((), (), s32[]{:S(2)}) async-start(), calls=%async_computation.3 | async-start | bytes 147456 | tf_op jit(solution)/shard_map/reduce_scatter | solution.py:50
  22.4 33.0 %copy-start.3 = (bf16[256,512]{1,0:T(8,128)(2,1)S(1)}, bf16[256,512]{1,0:T(8,128)(2,1)}, u32[]{:S(2)}) copy-start(bf16[256,512]{1,0:T(8,128)(2,1)} %param.14) | copy-start | bytes 786436
  22.4 33.0 %copy-start.9 = (f32[512]{0:T(512)S(1)}, f32[512]{0:T(512)}, u32[]{:S(2)}) copy-start(f32[512]{0:T(512)} %param.15) | copy-start | bytes 6148
  59.6 236.4 %all-reduce.6.cloned.1.call-start = ((), (), s32[]{:S(2)}) async-start(), calls=%async_computation.5 | async-start | bytes 13631488 | tf_op jit(solution)/shard_map/psum | solution.py:64
  123.2 5.7 %copy-start.4 = (f32[16,256]{1,0:T(8,128)S(1)}, f32[16,256]{1,0:T(8,128)}, u32[]{:S(2)}) copy-start(f32[16,256]{1,0:T(8,128)} %reduce-scatter.2.cloned.1.call-done) | copy-start | bytes 49156
  132.7 3.7 %copy-start.5 = (s32[1,8,4,32]{3,2,1,0:T(4,128)S(1)}, s32[1,8,4,32]{3,2,1,0:T(4,128)}, u32[]{:S(2)}) copy-start(s32[1,8,4,32]{3,2,1,0:T(4,128)} %param.16) | copy-start | bytes 12292
  132.7 15.1 %all-to-all-start.1 = ((f32[8,32,256]{2,1,0:T(8,128)}), f32[8,32,256]{2,1,0:T(8,128)S(1)}, u32[]{:S(2)}, u32[]{:S(2)}) async-start(f32[8,32,256]{2,1,0:T(8,128)} %bitcast.8), calls=%async_computation.2 | async-start | bytes 524288 | tf_op jit(solution)/shard_map/all_to_all | solution.py:51
  136.4 195.0 %all-reduce.4.cloned.1.call-start = ((), (), s32[]{:S(2)}) async-start(), calls=%async_computation.4 | async-start | bytes 524288 | tf_op jit(solution)/shard_map/psum | solution.py:65
  331.3 4.5 %copy-start.1 = (f32[256,512]{1,0:T(8,128)S(1)}, f32[256,512]{1,0:T(8,128)}, u32[]{:S(2)}) copy-start(f32[256,512]{1,0:T(8,128)} %get-tuple-element.34) | copy-start | bytes 1572868
  331.3 5.3 %copy-start.2 = (f32[256,256]{1,0:T(8,128)S(1)}, f32[256,256]{1,0:T(8,128)}, u32[]{:S(2)}) copy-start(f32[256,256]{1,0:T(8,128)} %all-reduce.4.cloned.1.call-done) | copy-start | bytes 786436
Sparse Core Ops, SparseCore 0:
  59.7 63.3 reduce-scatter.1
  132.8 163.1 all-reduce.5
  298.9 32.3 all-reduce.3
where the time goes:
time: 345 us; the launch traced here: 344 us
  waiting for transfers between devices  205 us (59%)
  blocking collectives  70.4 us (20%)
  local copies, waits for them, and re-layouts  16 us (5%)
  between operations  13.9 us (4%)
  matrix products  13.8 us (4%)
  other arithmetic  13.7 us (4%)
  starting transfers between devices  11.2 us (3%)
    psum x1, waiting for transfers between devices, body(): lax.psum((grad_tower_in, grad_tower_out, grad_inter, grad_out), ('grp', '...  99 us
    reduce_scatter x1, waiting for transfers between devices, body(): lax.psum_scatter(user_terms, 'tbl', scatter_dimension=0, tiled=True)  62.4 us
    psum x1, blocking collectives, body(): lax.psum((grad_tower_in, grad_tower_out, grad_inter, grad_out), ('grp', '...  39.4 us
    psum x1, waiting for transfers between devices, body(): grad_table = lax.psum(table_local, 'grp')  32.4 us
    all_gather x1, blocking collectives, body(): everyone = lax.all_gather(users, 'tbl', axis=0, tiled=True)  31 us
    all_to_all x1, waiting for transfers between devices, body(): lax.all_to_all(d_item.reshape(shards, slots, width), 'tbl', split_axis=0,...  11.1 us
    unnamed x26, local copies, waits for them, and re-layouts  8.96 us
    scatter-add x4, other arithmetic, body(): jax.ops.segment_sum(flat_back, local_ids[:, bag, :].reshape(-1), num_segm...  8.29 us
  transfers between devices with their start and end apart: 5, of which 4 were waited for; matrix products, arithmetic and copies ran while one was open for 5% of the time, Pallas kernels for 0%

commit v1 on v0

v1 whole, which is shorter than its diff:
```python
import functools
import math

import jax
import jax.numpy as jnp
from jax import lax
from jax.experimental import pallas as pl
from jax.experimental.pallas import tpu as pltpu
from jax.sharding import PartitionSpec as P

BF = jnp.bfloat16
F32 = jnp.float32
MESH = pl.DeviceIdType.MESH


def silu_slope(value):
    sig = jax.nn.sigmoid(value)
    return sig * (1.0 + value * (1.0 - sig))


def exchange_kernel(groups, shards, plan, *refs):
    count = len(plan)
    ins = refs[:count]
    outs = refs[count : 2 * count]
    send_sem, recv_sem, own_sem = refs[2 * count :]
    total = groups * shards
    my_grp = lax.axis_index("grp")
    my_tbl = lax.axis_index("tbl")
    me = my_grp * shards + my_tbl

    def size_of(scope):
        return {"all": total, "tbl": shards, "grp": groups}[scope]

    def place_of(scope):
        return {"all": me, "tbl": my_tbl, "grp": my_grp}[scope]

    def source(n, where):
        return ins[n].at[where] if plan[n][1] == "scatter" else ins[n]

    barrier = pltpu.get_barrier_semaphore()

    def greet(step, carry):
        peer = lax.rem(me + step, total)
        pl.semaphore_signal(
            barrier, inc=1, device_id=(peer // shards, peer % shards), device_id_type=MESH
        )
        return carry

    lax.fori_loop(1, total, greet, 0)
    for n, (scope, kind) in enumerate(plan):
        here = place_of(scope)
        pltpu.make_async_copy(source(n, here), outs[n].at[here], own_sem.at[n]).start()
    pl.semaphore_wait(barrier, total - 1)

    for wanted in ("tbl", "grp", "all"):
        chosen = [n for n in range(count) if plan[n][0] == wanted]
        if not chosen:
            continue
        size = size_of(wanted)
        here = place_of(wanted)

        def push(step, carry):
            there = lax.rem(here + step, size)
            if wanted == "all":
                target = (there // shards, there % shards)
            elif wanted == "tbl":
                target = (my_grp, there)
            else:
                target = (there, my_tbl)
            for n in chosen:
                pltpu.make_async_remote_copy(
                    src_ref=source(n, there),
                    dst_ref=outs[n].at[here],
                    send_sem=send_sem.at[n],
                    recv_sem=recv_sem.at[n],
                    device_id=target,
                    device_id_type=MESH,
                ).start()
            return carry

        lax.fori_loop(1, size, push, 0)
    for n, (scope, kind) in enumerate(plan):
        here = place_of(scope)
        others = outs[n].at[pl.ds(0, size_of(scope) - 1)]
        pltpu.make_async_copy(source(n, here), outs[n].at[here], own_sem.at[n]).wait()
        pltpu.make_async_copy(others, others, send_sem.at[n]).wait()
        pltpu.make_async_copy(others, others, recv_sem.at[n]).wait()


def exchange(ident, groups, shards, *items):
    plan = tuple((scope, kind) for scope, kind, _ in items)
    arrays = [array for _, _, array in items]
    sizes = {"all": groups * shards, "tbl": shards, "grp": groups}
    shapes = []
    for scope, kind, array in items:
        block = array.shape[1:] if kind == "scatter" else array.shape
        shapes.append(jax.ShapeDtypeStruct((sizes[scope],) + block, array.dtype))
    vmem = pl.BlockSpec(memory_space=pltpu.VMEM)
    return pl.pallas_call(
        functools.partial(exchange_kernel, groups, shards, plan),
        out_shape=shapes,
        in_specs=[vmem] * len(arrays),
        out_specs=[vmem] * len(arrays),
        scratch_shapes=[pltpu.SemaphoreType.DMA((len(arrays),))] * 3,
        compiler_params=pltpu.CompilerParams(collective_id=ident, has_side_effects=True),
        name="exchange_%d" % ident,
    )(*arrays)


def dot(a, b, ca, cb):
    return lax.dot_general(a, b, (((ca,), (cb,)), ((), ())), preferred_element_type=F32)


def body(
    user_feats, tower_in, tower_out, table, inter_weight, out_weight, ids, live, req_of, labels
):
    groups = lax.axis_size("grp")
    shards = lax.axis_size("tbl")
    total = groups * shards
    rows_table, width = table.shape
    slots = ids.shape[3]
    cands = shards * slots
    rows_user, feats = user_feats.shape
    group_rows = rows_user * shards
    units = inter_weight.shape[1]

    bags = jnp.swapaxes(ids[0], 1, 2).reshape(cands, -1)
    counts = jnp.sum(
        (bags[:, :, None] == jnp.arange(rows_table, dtype=jnp.int32)).astype(F32), axis=1
    ).astype(BF)
    pooled = dot(counts, table, 1, 0).astype(BF)
    items, all_feats = exchange(
        0,
        groups,
        shards,
        ("tbl", "scatter", pooled.reshape(shards, slots, width)),
        ("all", "gather", user_feats),
    )
    items = items.reshape(cands, width)
    all_feats = all_feats.reshape(total * rows_user, feats)
    group_feats = lax.dynamic_slice_in_dim(
        all_feats, lax.axis_index("grp") * group_rows, group_rows, 0
    )
    group_hidden = jax.nn.silu(dot(group_feats, tower_in, 1, 0)).astype(BF)
    users = dot(group_hidden, tower_out, 1, 0).astype(BF)
    request = req_of[0].reshape(-1)
    picks = (request[:, None] == jnp.arange(group_rows, dtype=jnp.int32)).astype(BF)
    chosen = dot(picks, users, 1, 0)
    items32 = items.astype(F32)
    cross = (items32 * chosen).astype(BF)
    inner = dot(cross, inter_weight, 1, 0)
    act = jax.nn.silu(inner)
    score = jnp.sum(act * out_weight, axis=1)
    factor = 1.0 / math.sqrt(groups * shards * shards * slots)
    slot_index = jnp.arange(slots, dtype=jnp.int32)
    mask = (slot_index[None, :] < live[0][:, None]).reshape(-1)
    target = labels[0].reshape(-1)
    grad_score = jnp.where(mask, jax.nn.sigmoid(score) - target, 0.0) * factor
    dinner = (grad_score[:, None] * out_weight * silu_slope(inner)).astype(BF)
    grad_inter = dot(cross, dinner, 0, 0).astype(BF)
    grad_out = jnp.sum(grad_score[:, None] * act, axis=0)
    dcross = dot(dinner, inter_weight, 1, 1)
    d_item = (dcross * chosen).astype(BF)
    d_user = (dcross * items32).astype(BF)
    user_terms = dot(picks, d_user, 0, 0).astype(BF)

    back, user_parts, inter_parts, out_parts = exchange(
        1,
        groups,
        shards,
        ("tbl", "scatter", d_item.reshape(shards, slots, width)),
        ("tbl", "scatter", user_terms.reshape(shards, rows_user, width)),
        ("all", "scatter", grad_inter.reshape(total, width // total, units)),
        ("all", "gather", grad_out.reshape(-1, 128)),
    )
    d_users_own = jnp.sum(user_parts.astype(F32), axis=0).astype(BF)
    inter_own = jnp.sum(inter_parts.astype(F32), axis=0).astype(BF)
    grad_out_total = jnp.sum(out_parts, axis=0).reshape(units)
    table_local = dot(counts, back.reshape(cands, width), 0, 0).astype(BF)

    table_parts, d_users, inter_all = exchange(
        2,
        groups,
        shards,
        ("grp", "gather", table_local),
        ("all", "gather", d_users_own),
        ("all", "gather", inter_own),
    )
    grad_table = jnp.sum(table_parts.astype(F32), axis=0)
    grad_inter_total = inter_all.reshape(width, units).astype(F32)
    d_users = d_users.reshape(total * rows_user, width)

    def tower_grads(part_feats, part_users):
        pre = dot(part_feats, tower_in, 1, 0)
        hidden = jax.nn.silu(pre).astype(BF)
        grad_out_part = dot(hidden, part_users, 0, 0)
        d_pre = (dot(part_users, tower_out, 1, 1) * silu_slope(pre)).astype(BF)
        return dot(part_feats, d_pre, 0, 0), grad_out_part

    rows_all = total * rows_user
    chunk = math.gcd(rows_all, 512)
    if chunk == rows_all:
        grad_tower_in, grad_tower_out = tower_grads(all_feats, d_users)
    else:

        def step(index, sums):
            one, two = tower_grads(
                lax.dynamic_slice_in_dim(all_feats, index * chunk, chunk, 0),
                lax.dynamic_slice_in_dim(d_users, index * chunk, chunk, 0),
            )
            return sums[0] + one, sums[1] + two

        grad_tower_in, grad_tower_out = lax.fori_loop(
            0,
            rows_all // chunk,
            step,
            (jnp.zeros(tower_in.shape, F32), jnp.zeros(tower_out.shape, F32)),
        )
    scores = score.reshape(1, shards, slots)
    return (scores, grad_tower_in, grad_tower_out, grad_inter_total, grad_out_total, grad_table)


def solution(mesh):
    placed = (
        P(("grp", "tbl"), None),
        P(),
        P(),
        P("tbl", None),
        P(),
        P(),
        P(("grp", "tbl"), None, None, None),
        P(("grp", "tbl"), None),
        P(("grp", "tbl"), None, None),
        P(("grp", "tbl"), None, None),
    )
    return jax.shard_map(
        body,
        mesh=mesh,
        in_specs=placed,
        out_specs=(P(("grp", "tbl"), None, None), P(), P(), P(), P(), P("tbl", None)),
        check_vma=False,
    )
```

time: 345 us -> 107 us (0.31)
  waiting for transfers between devices: 205 us -> 0 us
  blocking collectives: 70.4 us -> 0 us
  Pallas kernels: 0 us -> 52.9 us
  matrix products: 13.8 us -> 38.6 us
  between operations: 13.9 us -> 0.7 us
  local copies, waits for them, and re-layouts: 16 us -> 3.77 us
  starting transfers between devices: 11.2 us -> 0 us
    psum x2 -> x0, waiting for transfers between devices: 131 us -> none  [the longest x1 99 us: body(): lax.psum((grad_tower_in, grad_tower_out, grad_inter, grad_out), ('grp', '...]
    reduce_scatter x1 -> x0, waiting for transfers between devices: 62.4 us -> none  [body(): lax.psum_scatter(user_terms, 'tbl', scatter_dimension=0, tiled=True)]
    pallas_call x0 -> x3, Pallas kernels: none -> 52.9 us  [exchange(): pl.pallas_call(functools.partial(exchange_kernel, groups, shards, plan),...]
    psum x1 -> x0, blocking collectives: 39.4 us -> none  [body(): lax.psum((grad_tower_in, grad_tower_out, grad_inter, grad_out), ('grp', '...]
    all_gather x1 -> x0, blocking collectives: 31 us -> none  [body(): everyone = lax.all_gather(users, 'tbl', axis=0, tiled=True)]
    dot_general x8 -> x11, matrix products: 13.8 us -> 38.6 us  [dot(): lax.dot_general(a, b, (((ca,), (cb,)), ((), ())), preferred_element_type=...]
    all_to_all x2 -> x0, waiting for transfers between devices: 11.1 us -> none  [the longest x1 11.1 us: body(): lax.all_to_all(d_item.reshape(shards, slots, width), 'tbl', split_axis=0,...]
    all_to_all x2 -> x0, starting transfers between devices: 11.1 us -> none  [the longest x1 7.41 us: body(): lax.all_to_all(pooled, 'tbl', split_axis=0, concat_axis=0, tiled=True)]
  transfers between devices with their start and end apart: 5 -> 0, of which waited for: 4 -> 0; matrix products, arithmetic and copies ran while one was open for 5% -> 0% of each run, Pallas kernels for 0% -> 0%
where the time goes in v1:
time: 107 us
  Pallas kernels  52.9 us (49%)
  matrix products  38.6 us (36%)
  other arithmetic  10.6 us (10%)
  local copies, waits for them, and re-layouts  3.77 us (4%)
    pallas_call x3, Pallas kernels, exchange(): pl.pallas_call(functools.partial(exchange_kernel, groups, shards, plan),...  52.9 us
    dot_general x11, matrix products, dot(): lax.dot_general(a, b, (((ca,), (cb,)), ((), ())), preferred_element_type=...  38.6 us

profile of v1, /device:TPU:0, one launch (start us, length us, event | category | flops | bytes accessed | tf_op | source)
XLA Modules:
  0.0 106.6 jit_solution(11205617347873811114)
XLA Ops:
  0.6 0.0 copy-start
  0.7 0.9 eq.34
  1.6 0.7 iota_compare_fusion.4
  2.3 0.6 lt.31
  2.9 0.8 reshape_squeeze.3
  3.7 0.7 copy.18
  4.4 0.1 eq.30
  4.5 0.2 convert_reduce_fusion.1
  4.7 1.8 %convolution_convert_fusion.2 = bf16[256,256]{1,0:T(8,128)(2,1)} fusion(bf16[256,256]{1,0:T(8,128)(2,1)} %param.13, bf16[256,256]{1,0:T(8,128)(2,1)S(1)} %convert_reduce_fusion.1), kind=kOutput, calls=%fused_computation.9 | convolution fusion | flops 33619968 | bytes 393216 | tf_op jit(solution)/shard_map/dot_general | solution.py:111
  6.4 15.8 %exchange_0.1 = (bf16[8,32,256]{2,1,0:T(8,128)(2,1)}, bf16[32,16,128]{2,1,0:T(8,128)(2,1)}) custom-call(bf16[8,32,256]{2,1,0:T(8,128)(2,1)} %bitcast.41, bf16[16,128]{1,0:T(8,128)(2,1)} %refs_1_.1), custom_call_target="tpu_custom_call" | custom-call | tf_op jit(solution)/shard_map/exchange_0/pallas_call | solution.py:99
  22.2 3.0 %fusion.12 = f32[128,4096]{1,0:T(8,128)} fusion(bf16[128,4096]{1,0:T(8,128)(2,1)} %param.11, bf16[512,128]{1,0:T(8,128)(2,1)} %bitcast.43, s32[]{:T(128)S(6)} %select_n.11), kind=kOutput, calls=%fused_computation.32 | convolution fusion | flops 134217728 | bytes 3178500 | tf_op jit(solution)/shard_map/dot_general | solution.py:111
  25.2 0.0 copy-done
  25.2 3.3 %fusion.5 = (bf16[256,256]{1,0:T(8,128)(2,1)}, f32[256,256]{1,0:T(8,128)}) fusion(bf16[8,32,256]{2,1,0:T(8,128)(2,1)} %get-tuple-element.15, bf16[4096,256]{1,0:T(8,128)(2,1)S(1)} %copy-done, f32[128,4096]{1,0:T(8,128)} %fusion.12, s32[256]{0:T(256)S(1)} %eq.34), kind=kOutput, calls=%fused_computation.23 | convolution fusion | flops 288096256 | bytes 4719616 | tf_op jit(solution)/shard_map/dot_general | solution.py:111
  28.5 1.4 %multiply_reduce_fusion.1 = (f32[256]{0:T(256)S(1)}, f32[256,512]{1,0:T(8,128)S(1)}) fusion(f32[512]{0:T(512)S(1)} %copy-done.4, bf16[256,256]{1,0:T(8,128)(2,1)} %get-tuple-element.26, bf16[256,512]{1,0:T(8,128)(2,1)S(1)} %copy-done.2), kind=kOutput, calls=%fused_computation.18 | convolution fusion | flops 67895040 | bytes 920576 | tf_op jit(solution)/shard_map/dot_general | solution.py:111
  29.8 0.7 select_multiply_fusion
  30.5 0.9 multiply_reduce_fusion
  31.4 0.7 reshape.80
  32.1 1.9 %fusion.2.refs_2_ = bf16[32,8,512]{2,1,0:T(8,128)(2,1)} fusion(bf16[256,256]{1,0:T(8,128)(2,1)} %get-tuple-element.26, bf16[256,512]{1,0:T(8,128)(2,1)S(1)} %get-tuple-element.25), kind=kOutput, calls=%fused_computation.7 | convolution fusion | flops 67239936 | bytes 655360 | tf_op jit(solution)/shard_map/dot_general | solution.py:111
  33.9 1.9 %multiply_convert_fusion.7 = (bf16[256,256]{1,0:T(8,128)(2,1)}, f32[256,256]{1,0:T(8,128)S(1)}) fusion(f32[256,256]{1,0:T(8,128)} %get-tuple-element.27, bf16[256,512]{1,0:T(8,128)(2,1)S(1)} %get-tuple-element.25, bf16[256,512]{1,0:T(8,128)(2,1)} %param.14), kind=kOutput, calls=%fused_computation.26 | convolution fusion | flops 67239936 | bytes 1179648 | tf_op jit(solution)/shard_map/dot_general | solution.py:111
  35.9 1.8 %convolution_convert_fusion.4 = bf16[128,256]{1,0:T(8,128)(2,1)} fusion(f32[256,256]{1,0:T(8,128)S(1)} %get-tuple-element.31, bf16[256,256]{1,0:T(8,128)(2,1)} %bitcast.46, s32[256]{0:T(256)S(1)} %eq.34), kind=kOutput, calls=%fused_computation.11 | convolution fusion | flops 17039360 | bytes 459776 | tf_op jit(solution)/shard_map/dot_general | solution.py:111
  37.7 18.6 %exchange_1.1 = (bf16[8,32,256]{2,1,0:T(8,128)(2,1)}, bf16[8,16,256]{2,1,0:T(8,128)(2,1)}, bf16[32,8,512]{2,1,0:T(8,128)(2,1)}, f32[32,4,128]{2,1,0:T(4,128)}) custom-call(bf16[8,32,256]{2,1,0:T(8,128)(2,1)} %bitcast.40, bf16[8,16,256]{2,1,0:T(8,128)(2,1)} %bitcast.42, bf16[32,8,512]{2,1,0:T(8,128)(2,1)} %fusion.2.refs_2_, f32[4,128]{1,0:T(4,128)} %bitcast.49), custom_call_target="tpu_custom_call" | custom-call | tf_op jit(solution)/shard_map/exchange_1/pallas_call | solution.py:99
  56.3 1.8 %convolution_convert_fusion.1.refs_0_ = bf16[256,256]{1,0:T(8,128)(2,1)} fusion(bf16[256,256]{1,0:T(8,128)(2,1)} %bitcast.47, bf16[256,256]{1,0:T(8,128)(2,1)S(1)} %convert_reduce_fusion.1), kind=kOutput, calls=%fused_computation.8 | convolution fusion | flops 33619968 | bytes 393216 | tf_op jit(solution)/shard_map/dot_general | solution.py:111
  58.1 1.5 %reduce_sum.74 = f32[4,128]{1,0:T(4,128)} reduce(f32[32,4,128]{2,1,0:T(4,128)} %get-tuple-element.22, f32[]{:T(128)} %constant.8.clone.1), dimensions={0}, to_apply=%region_5.6 | reduce | flops 15872 | bytes 67588 | tf_op jit(solution)/shard_map/reduce_sum | solution.py:178
  59.6 1.5 %reduce_sum.72.refs_1_ = bf16[16,256]{1,0:T(8,128)(2,1)} reduce(bf16[8,16,256]{2,1,0:T(8,128)(2,1)} %get-tuple-element.18, bf16[]{:T(256)} %constant.27.clone.1), dimensions={0}, to_apply=%region_3.4 | reduce | flops 28672 | bytes 73730 | tf_op jit(solution)/shard_map/reduce_sum | solution.py:176
  61.0 1.6 %reduce_sum.73.refs_2_ = bf16[8,512]{1,0:T(8,128)(2,1)} reduce(bf16[32,8,512]{2,1,0:T(8,128)(2,1)} %get-tuple-element.19, bf16[]{:T(256)} %constant.27.clone.1), dimensions={0}, to_apply=%region_4.5 | reduce | flops 126976 | bytes 270338 | tf_op jit(solution)/shard_map/reduce_sum | solution.py:177
  62.6 18.5 %exchange_2.1 = (bf16[4,256,256]{2,1,0:T(8,128)(2,1)}, bf16[32,16,256]{2,1,0:T(8,128)(2,1)}, bf16[32,8,512]{2,1,0:T(8,128)(2,1)}) custom-call(bf16[256,256]{1,0:T(8,128)(2,1)} %convolution_convert_fusion.1.refs_0_, bf16[16,256]{1,0:T(8,128)(2,1)} %reduce_sum.72.refs_1_, bf16[8,512]{1,0:T(8,128)(2,1)} %reduce_sum.73.refs_2_), custom_call_target="tpu_custom_call" | custom-call | tf_op jit(solution)/shard_map/exchange_2/pallas_call | solution.py:99
  81.2 1.8 %convert_reduce_fusion = f32[256,256]{1,0:T(8,128)} fusion(bf16[4,256,256]{2,1,0:T(8,128)(2,1)} %get-tuple-element.23), kind=kLoop, calls=%fused_computation.13 | loop fusion | flops 458752 | bytes 786432 | tf_op jit(solution)/shard_map/reduce_sum | solution.py:189
  83.0 1.8 %bitcast_convert_fusion = f32[256,512]{1,0:T(8,128)} fusion(bf16[32,8,512]{2,1,0:T(8,128)(2,1)} %get-tuple-element.21), kind=kLoop, calls=%fused_computation.25 | loop fusion | flops 131072 | bytes 786432 | tf_op jit(solution)/shard_map/convert_element_type | solution.py:190
  84.8 0.0 copy-done.1
  84.8 5.4 %fusion.19 = f32[512,4096]{1,0:T(8,128)} fusion(bf16[512,128]{1,0:T(8,128)(2,1)} %bitcast.44, bf16[128,4096]{1,0:T(8,128)(2,1)S(1)} %copy-done.1), kind=kOutput, calls=%fused_computation.41 | convolution fusion | flops 536870912 | bytes 9568256 | tf_op jit(solution)/shard_map/dot_general | solution.py:111
  90.2 8.5 %fusion.1 = f32[128,4096]{1,0:T(8,128)} fusion(bf16[512,128]{1,0:T(8,128)(2,1)S(1)} %bitcast.45, f32[512,4096]{1,0:T(8,128)} %fusion.19, bf16[512,256]{1,0:T(8,128)(2,1)S(1)} %bitcast.51, bf16[4096,256]{1,0:T(8,128)(2,1)S(1)} %copy-done), kind=kOutput, calls=%fused_computation.5 | convolution fusion | flops 1629487104 | bytes 12976128 | tf_op jit(solution)/shard_map/dot_general | solution.py:111
  98.8 7.8 %fusion = f32[4096,256]{1,0:T(8,128)} fusion(bf16[512,256]{1,0:T(8,128)(2,1)S(1)} %bitcast.52, f32[512,4096]{1,0:T(8,128)} %fusion.19), kind=kOutput, calls=%fused_computation.3 | convolution fusion | flops 1084227584 | bytes 12845056 | tf_op jit(solution)/shard_map/dot_general | solution.py:111
  (9 shorter events, 0.0 us)
Async XLA Ops:
  0.6 24.6 %copy-start = (bf16[4096,256]{1,0:T(8,128)(2,1)S(1)}, bf16[4096,256]{1,0:T(8,128)(2,1)}, u32[]{:S(2)}) copy-start(bf16[4096,256]{1,0:T(8,128)(2,1)} %param.12) | copy-start | bytes 6291460
  25.2 3.3 %copy-start.2 = (bf16[256,512]{1,0:T(8,128)(2,1)S(1)}, bf16[256,512]{1,0:T(8,128)(2,1)}, u32[]{:S(2)}) copy-start(bf16[256,512]{1,0:T(8,128)(2,1)} %param.14) | copy-start | bytes 786436
  25.2 3.3 %copy-start.4 = (f32[512]{0:T(512)S(1)}, f32[512]{0:T(512)}, u32[]{:S(2)}) copy-start(f32[512]{0:T(512)} %param.15) | copy-start | bytes 6148
  28.5 56.3 %copy-start.1 = (bf16[128,4096]{1,0:T(8,128)(2,1)S(1)}, bf16[128,4096]{1,0:T(8,128)(2,1)}, u32[]{:S(2)}) copy-start(bf16[128,4096]{1,0:T(8,128)(2,1)} %param.11) | copy-start | bytes 3145732
  84.8 5.4 %copy-start.3 = (bf16[32,16,128]{2,1,0:T(8,128)(2,1)S(1)}, bf16[32,16,128]{2,1,0:T(8,128)(2,1)}, u32[]{:S(2)}) copy-start(bf16[32,16,128]{2,1,0:T(8,128)(2,1)} %get-tuple-element.16) | copy-start | bytes 393220
  84.8 5.4 %copy-start.5 = (bf16[32,16,256]{2,1,0:T(8,128)(2,1)S(1)}, bf16[32,16,256]{2,1,0:T(8,128)(2,1)}, u32[]{:S(2)}) copy-start(bf16[32,16,256]{2,1,0:T(8,128)(2,1)} %get-tuple-element.20) | copy-start | bytes 786436

commit v2 on v0

v2 whole, which is shorter than its diff:
```python
import functools
import math

import jax
import jax.numpy as jnp
from jax import lax
from jax.experimental import pallas as pl
from jax.experimental.pallas import tpu as pltpu
from jax.sharding import PartitionSpec as P

BF = jnp.bfloat16
F32 = jnp.float32
MESH = pl.DeviceIdType.MESH


def silu_slope(value):
    sig = jax.nn.sigmoid(value)
    return sig * (1.0 + value * (1.0 - sig))


def dot(a, b, ca, cb):
    return lax.dot_general(a, b, (((ca,), (cb,)), ((), ())), preferred_element_type=F32)


def step_kernel(groups, shards, slots, bags, tile, in_place, *refs):
    refs = list(refs)
    take = lambda n: [refs.pop(0) for _ in range(n)]
    feats, t_in, t_out, table, weight, out_w, cols, rows = take(8)
    scores, g_inter, g_out, g_table, tower_a, tower_b = take(6)
    pool_s, pool_r, feat_r, item_s, item_r, term_s, term_r = take(7)
    inter_s, inter_r, out_s, out_r, mine_s, users_r, part_s, part_r, sum_s, sum_r = take(10)
    if in_place:
        t_in_t, hidden_t, slope_t = take(3)
    send_sem, recv_sem, own_sem = take(3)
    total = groups * shards
    my_grp = lax.axis_index("grp")
    my_tbl = lax.axis_index("tbl")
    me = my_grp * shards + my_tbl
    rows_table, width = table.shape
    hidden_width = t_out.shape[0]
    units = weight.shape[1]
    cands = cols.shape[0]
    rows_user = feats.shape[0]
    group_rows = shards * rows_user
    sizes = {"all": total, "tbl": shards, "grp": groups, "far": total - shards + 1}
    places = {"all": me, "tbl": my_tbl, "grp": my_grp}
    links = {
        "pool": (0, "tbl", pool_s, pool_r, True),
        "near": (1, "tbl", feats, feat_r, False),
        "far": (2, "far", feats, feat_r, False),
        "item": (3, "tbl", item_s, item_r, True),
        "term": (4, "tbl", term_s, term_r, True),
        "inter": (5, "all", inter_s, inter_r, True),
        "out": (6, "all", out_s, out_r, False),
        "mine": (7, "all", mine_s, users_r, False),
        "part": (8, "grp", part_s, part_r, False),
        "sum": (9, "all", sum_s, sum_r, False),
    }

    def spot(name):
        return me if name in ("near", "far") else places[links[name][1]]

    def origin(name, where):
        _, _, source, _, scatter = links[name]
        return source.at[where] if scatter else source

    def own(name):
        sem, _, _, target, _ = links[name]
        here = spot(name)
        return pltpu.make_async_copy(origin(name, here), target.at[here], own_sem.at[sem])

    def push(*names):
        scope = links[names[0]][1]
        for name in names:
            if name != "far":
                own(name).start()

        def one(step, carry):
            if scope == "all":
                there = lax.rem(me + step, total)
                device = (there // shards, there % shards)
            elif scope == "tbl":
                there = lax.rem(my_tbl + step, shards)
                device = (my_grp, there)
            elif scope == "grp":
                there = lax.rem(my_grp + step, groups)
                device = (there, my_tbl)
            else:
                there = lax.rem((my_grp + 1) * shards + step - 1, total)
                device = (there // shards, there % shards)
            for name in names:
                sem, _, _, target, _ = links[name]
                pltpu.make_async_remote_copy(
                    src_ref=origin(name, there),
                    dst_ref=target.at[spot(name)],
                    send_sem=send_sem.at[sem],
                    recv_sem=recv_sem.at[sem],
                    device_id=device,
                    device_id_type=MESH,
                ).start()
            return carry

        lax.fori_loop(1, sizes[scope], one, 0)

    def others(name):
        _, scope, _, target, _ = links[name]
        return target.at[pl.ds(0, sizes[scope] - 1)]

    def arrive(name):
        if name != "far":
            own(name).wait()
        pltpu.make_async_copy(others(name), others(name), recv_sem.at[links[name][0]]).wait()

    barrier = pltpu.get_barrier_semaphore()

    def greet(step, carry):
        peer = lax.rem(me + step, total)
        pl.semaphore_signal(
            barrier, inc=1, device_id=(peer // shards, peer % shards), device_id_type=MESH
        )
        return carry

    lax.fori_loop(1, total, greet, 0)

    lane = lax.broadcasted_iota(jnp.int32, (cands, rows_table), 1).astype(F32)
    counts = jnp.zeros((cands, rows_table), F32)
    for bag in range(bags):
        counts = counts + jnp.where(cols[:, bag : bag + 1] == lane, 1.0, 0.0)
    pooled = dot(counts.astype(BF), table[...], 1, 0)
    pool_s[...] = pooled.reshape(shards, slots, width).astype(BF)
    pl.semaphore_wait(barrier, total - 1)
    push("near", "pool")
    push("far")
    if in_place:

        def flip(index, carry):
            at = pl.ds(pl.multiple_of(index * tile, tile), tile)
            t_in_t[at, :] = t_in[:, at].T
            return carry

        lax.fori_loop(0, hidden_width // tile, flip, 0)

    arrive("near")
    group_feats = feat_r[pl.ds(my_grp * shards, shards)].reshape(group_rows, -1)

    def forward(index, acc):
        at = pl.ds(pl.multiple_of(index * tile, tile), tile)
        pre = dot(group_feats, t_in[:, at], 1, 0)
        hidden = (pre * jax.nn.sigmoid(pre)).astype(BF)
        return acc + dot(hidden, t_out[at, :], 1, 0)

    users = lax.fori_loop(
        0, hidden_width // tile, forward, jnp.zeros((group_rows, width), F32)
    ).astype(BF)
    lane = lax.broadcasted_iota(jnp.int32, (cands, group_rows), 1).astype(F32)
    picks = jnp.where(cols[:, bags : bags + 1] == lane, 1.0, 0.0).astype(BF)
    chosen = dot(picks, users, 1, 0)
    arrive("pool")
    items = pool_r[...].reshape(cands, width).astype(F32)
    cross = (items * chosen).astype(BF)
    inner = dot(cross, weight[...], 1, 0)
    sig = jax.nn.sigmoid(inner)
    act = inner * sig
    score = jnp.sum(act * out_w[...], axis=1, keepdims=True)
    scores[...] = score
    factor = 1.0 / math.sqrt(groups * shards * shards * slots)
    grad = cols[:, bags + 1 : bags + 2] * (jax.nn.sigmoid(score) - cols[:, bags + 2 : bags + 3]) * factor
    slope = sig * (1.0 + inner * (1.0 - sig))
    dinner = (grad * out_w[...] * slope).astype(BF)
    dcross = dot(dinner, weight[...], 1, 1)
    item_s[...] = (dcross * chosen).reshape(shards, slots, width).astype(BF)
    side = lax.broadcasted_iota(jnp.int32, (group_rows, cands), 0).astype(F32)
    picks_t = jnp.where(rows[bags : bags + 1, :] == side, 1.0, 0.0).astype(BF)
    terms = dot(picks_t, (dcross * items).astype(BF), 1, 0)
    term_s[...] = terms.reshape(shards, rows_user, width).astype(BF)
    push("term", "item")
    out_s[...] = jnp.sum(grad * act, axis=0, keepdims=True)
    inter = dot(cross, dinner, 0, 0)
    inter_s[...] = inter.reshape(total, width // total, units).astype(BF)
    push("inter", "out")
    arrive("far")
    all_rows = total * rows_user
    if in_place:
        all_feats = feat_r[...].reshape(all_rows, -1)

        def ahead(index, carry):
            at = pl.ds(pl.multiple_of(index * tile, tile), tile)
            pre = dot(t_in_t[at, :], all_feats, 1, 1)
            gate = jax.nn.sigmoid(pre)
            hidden_t[at, :] = (pre * gate).astype(BF)
            slope_t[at, :] = (gate * (1.0 + pre * (1.0 - gate))).astype(BF)
            return carry

        lax.fori_loop(0, hidden_width // tile, ahead, 0)
    arrive("term")
    mine_s[...] = jnp.sum(term_r[...].astype(F32), axis=0).astype(BF)
    push("mine")
    arrive("item")
    side = lax.broadcasted_iota(jnp.int32, (rows_table, cands), 0).astype(F32)
    counts_t = jnp.zeros((rows_table, cands), F32)
    for bag in range(bags):
        counts_t = counts_t + jnp.where(rows[bag : bag + 1, :] == side, 1.0, 0.0)
    part_s[...] = dot(counts_t.astype(BF), item_r[...].reshape(cands, width), 1, 0).astype(BF)
    push("part")
    arrive("inter")
    sum_s[...] = jnp.sum(inter_r[...].astype(F32), axis=0).astype(BF)
    push("sum")
    arrive("out")
    g_out[...] = jnp.sum(out_r[...], axis=0)
    arrive("mine")
    if in_place:
        d_users = users_r[...].reshape(all_rows, width)
        d_users_t = d_users.T
        feats_t = all_feats.T

        def behind(index, carry):
            at = pl.ds(pl.multiple_of(index * tile, tile), tile)
            tower_b[at, :] = dot(hidden_t[at, :], d_users, 1, 0)
            d_hidden = dot(t_out[at, :], d_users_t, 1, 0)
            d_pre = (d_hidden * slope_t[at, :].astype(F32)).astype(BF)
            tower_a[:, at] = dot(feats_t, d_pre, 1, 1)
            return carry

        lax.fori_loop(0, hidden_width // tile, behind, 0)
    else:
        tower_a[...] = feat_r[...]
        tower_b[...] = users_r[...]
    arrive("part")
    g_table[...] = jnp.sum(part_r[...].astype(F32), axis=0)
    arrive("sum")
    g_inter[...] = sum_r[...].astype(F32)
    for name in links:
        pltpu.make_async_copy(others(name), others(name), send_sem.at[links[name][0]]).wait()


def body(
    user_feats, tower_in, tower_out, table, inter_weight, out_weight, ids, live, req_of, labels
):
    groups = lax.axis_size("grp")
    shards = lax.axis_size("tbl")
    total = groups * shards
    rows_table, width = table.shape
    slots = ids.shape[3]
    cands = shards * slots
    rows_user, feats = user_feats.shape
    hidden_width = tower_out.shape[0]
    units = inter_weight.shape[1]
    rows_all = total * rows_user
    tile = math.gcd(hidden_width, 512)
    in_place = rows_all <= 512

    slot_index = jnp.arange(slots, dtype=jnp.int32)
    mask = (slot_index[None, :] < live[0][:, None]).reshape(1, cands)
    rows = jnp.concatenate(
        [
            jnp.swapaxes(ids[0], 0, 1).reshape(-1, cands).astype(F32),
            req_of[0].reshape(1, cands).astype(F32),
            mask.astype(F32),
            labels[0].reshape(1, cands),
            jnp.zeros((1, cands), F32),
        ]
    )
    struct = jax.ShapeDtypeStruct
    outs = [
        struct((cands, 1), F32),
        struct((total, width // total, units), F32),
        struct((1, units), F32),
        struct((rows_table, width), F32),
    ]
    if in_place:
        outs += [struct(tower_in.shape, F32), struct(tower_out.shape, F32)]
    else:
        outs += [struct((total, rows_user, feats), BF), struct((total, rows_user, width), BF)]
    blocks = (shards, slots, width)
    terms = (shards, rows_user, width)
    inter = (total, width // total, units)
    buffers = [
        (blocks, BF), (blocks, BF), ((total, rows_user, feats), BF),
        (blocks, BF), (blocks, BF), (terms, BF), (terms, BF),
        (inter, BF), (inter, BF), ((1, units), F32), ((total, 1, units), F32),
        ((rows_user, width), BF), ((total, rows_user, width), BF),
        ((rows_table, width), BF), ((groups, rows_table, width), BF),
        (inter[1:], BF), (inter, BF),
    ]
    if in_place:
        buffers += [
            ((hidden_width, feats), BF),
            ((hidden_width, rows_all), BF),
            ((hidden_width, rows_all), BF),
        ]
    vmem = pl.BlockSpec(memory_space=pltpu.VMEM)
    score, inter_total, out_total, grad_table, first, second = pl.pallas_call(
        functools.partial(step_kernel, groups, shards, slots, ids.shape[2], tile, in_place),
        out_shape=outs,
        in_specs=[vmem] * 8,
        out_specs=[vmem] * 6,
        scratch_shapes=[pltpu.VMEM(shape, kind) for shape, kind in buffers]
        + [pltpu.SemaphoreType.DMA((10,))] * 3,
        compiler_params=pltpu.CompilerParams(
            collective_id=0, has_side_effects=True, vmem_limit_bytes=60 * 1024 * 1024
        ),
        name="ranking_step",
    )(
        user_feats, tower_in, tower_out, table, inter_weight,
        out_weight.reshape(1, units), rows.T, rows,
    )

    def tower_grads(part_feats, part_users):
        pre = dot(part_feats, tower_in, 1, 0)
        hidden = jax.nn.silu(pre).astype(BF)
        grad_out_part = dot(hidden, part_users, 0, 0)
        d_pre = (dot(part_users, tower_out, 1, 1) * silu_slope(pre)).astype(BF)
        return dot(part_feats, d_pre, 0, 0), grad_out_part

    if not in_place:
        all_feats = first.reshape(rows_all, feats)
        d_users = second.reshape(rows_all, width)
        chunk = math.gcd(rows_all, 512)

        def step(index, sums):
            one, two = tower_grads(
                lax.dynamic_slice_in_dim(all_feats, index * chunk, chunk, 0),
                lax.dynamic_slice_in_dim(d_users, index * chunk, chunk, 0),
            )
            return sums[0] + one, sums[1] + two

        first, second = lax.fori_loop(
            0,
            rows_all // chunk,
            step,
            (jnp.zeros(tower_in.shape, F32), jnp.zeros(tower_out.shape, F32)),
        )
    return (
        score.reshape(1, shards, slots),
        first,
        second,
        inter_total.reshape(width, units),
        out_total.reshape(units),
        grad_table,
    )


def solution(mesh):
    placed = (
        P(("grp", "tbl"), None),
        P(),
        P(),
        P("tbl", None),
        P(),
        P(),
        P(("grp", "tbl"), None, None, None),
        P(("grp", "tbl"), None),
        P(("grp", "tbl"), None, None),
        P(("grp", "tbl"), None, None),
    )
    return jax.shard_map(
        body,
        mesh=mesh,
        in_specs=placed,
        out_specs=(P(("grp", "tbl"), None, None), P(), P(), P(), P(), P("tbl", None)),
        check_vma=False,
    )
```

time: 345 us -> 59.8 us (0.17)
  the two profiles are of different devices: /device:TPU:0 before, /device:TPU:29 now
where the time goes in v2:
time: 59.8 us; the launch traced here: 59.5 us
  Pallas kernels  45.8 us (77%)
  local copies, waits for them, and re-layouts  9.88 us (17%)
  other arithmetic  3.14 us (5%)
  between operations  0.67 us (1%)
    pallas_call x1, Pallas kernels, body(): pl.pallas_call(functools.partial(step_kernel, groups, shards, slots, ids....  45.8 us
    unnamed x15, local copies, waits for them, and re-layouts  7.37 us

profile of v2, /device:TPU:29, one launch (start us, length us, event | category | flops | bytes accessed | tf_op | source)
XLA Modules:
  0.0 59.5 jit_solution(11507841151076801227)
XLA Ops:
  0.6 0.8 %reshape_squeeze.4 = f32[1,256]{1,0:T(1,128)S(1)} reshape(f32[1,8,32]{2,1,0:T(8,128)} %param.19) | data formatting | bytes 2048 | tf_op jit(solution)/shard_map/reshape;squeeze | solution.py:259
  1.4 0.7 %fusion = f32[8,32]{1,0:T(8,128)S(1)} fusion(s32[8]{0:T(128)} %bitcast.13), kind=kLoop, calls=%fused_computation.2 | loop fusion | flops 512 | bytes 1056 | tf_op jit(solution)/shard_map/convert_element_type | solution.py:258
  2.1 0.1 reshape.73
  2.2 0.7 %convert_element_type.44 = f32[1,8,32]{2,1,0:T(8,128)S(1)} convert(s32[1,8,32]{2,1,0:T(8,128)} %param.18) | non-fusion elementwise | flops 256 | bytes 2048 | tf_op jit(solution)/shard_map/convert_element_type | solution.py:257
  2.9 0.1 convert_element_type.45
  3.0 0.7 %convert_bitcast_fusion = f32[4,8,32]{2,0,1:T(4,128)S(1)} fusion(s32[1,8,4,32]{3,2,1,0:T(4,128)} %param.16), kind=kLoop, calls=%fused_computation | loop fusion | flops 1024 | bytes 8192 | tf_op jit(solution)/shard_map/convert_element_type | solution.py:256
  3.7 0.1 convert_element_type.43
  3.8 0.0 copy-start.3
  3.8 0.8 %copy.19.refs_6_ = f32[256,8]{1,0:T(8,128)} copy(f32[256,8]{0,1:T(8,128)S(1)} %bitcast.10) | data formatting | bytes 16384 | tf_op jit(solution)/shard_map/transpose | solution.py:305
  4.6 0.0 copy-done.3
  4.6 45.8 %ranking_step.1 = (f32[256,1]{1,0:T(8,128)}, f32[32,8,512]{2,1,0:T(8,128)}, f32[1,512]{1,0:T(1,128)}, f32[256,256]{1,0:T(8,128)}, f32[128,4096]{1,0:T(8,128)}, /*index=5*/f32[4096,256]{1,0:T(8,128)}) custom-call(bf16[16,128]{1,0:T(8,128)(2,1)} %refs_0_.1, bf16[128,4096]{1,0:T(8,128)(2,1)} %refs_1_.1, bf16[4096,256]{1,0:T(8,128)(2,1)} %refs_2_.1, ...), custom_call_target="tpu_custom_call" | custom-call | tf_op jit(solution)/shard_map/ranking_step/pallas_call | solution.py:292
  50.4 1.0 %reduce = f32[256]{0:T(256)S(1)} reduce(f32[256,1]{1,0:T(8,128)} %get-tuple-element.12, f32[]{:T(128)} %constant.7), dimensions={1}, to_apply=%get-tuple-element.12.reduce_sub_computation | reduce | bytes 2052 | tf_op jit(solution)/shard_map/ranking_step/pallas_call | solution.py:292
  51.4 0.7 %reshape.70 = f32[1,8,32]{2,1,0:T(8,128)} reshape(f32[256]{0:T(256)S(1)} %reduce) | data formatting | bytes 2048 | tf_op jit(solution)/shard_map/reshape | solution.py:334
  52.1 0.0 copy-start
  52.1 3.3 %copy.25 = f32[128,4096]{1,0:T(8,128)} copy(f32[128,4096]{1,0:T(8,128)} %get-tuple-element.25) | data formatting | bytes 4194304
  55.4 0.0 copy-done
  55.4 0.0 copy-start.1
  55.4 0.0 copy-start.4
  55.4 0.0 copy-start.2
  55.4 2.0 %copy.26 = f32[4096,256]{1,0:T(8,128)} copy(f32[4096,256]{1,0:T(8,128)S(1)} %copy-done) | data formatting | bytes 8388608
  57.4 0.0 copy-done.1
  57.4 0.8 %copy.27 = f32[256,512]{1,0:T(8,128)} copy(f32[256,512]{1,0:T(8,128)S(1)} %bitcast.9) | data formatting | bytes 1048576
  58.2 0.0 copy-done.4
  58.2 0.6 copy.28
  58.8 0.0 copy-done.2
  58.8 0.7 %copy.29 = f32[256,256]{1,0:T(8,128)} copy(f32[256,256]{1,0:T(8,128)S(1)} %copy-done.2) | data formatting | bytes 524288
  (3 shorter events, 0.0 us)
Async XLA Ops:
  3.8 0.8 %copy-start.3 = (f32[8,256]{1,0:T(8,128)}, f32[8,256]{1,0:T(8,128)S(1)}, u32[]{:S(2)}) copy-start(f32[8,256]{1,0:T(8,128)S(1)} %concatenate.3.refs_7_) | copy-start | bytes 24580
  52.1 3.3 %copy-start = (f32[4096,256]{1,0:T(8,128)S(1)}, f32[4096,256]{1,0:T(8,128)}, u32[]{:S(2)}) copy-start(f32[4096,256]{1,0:T(8,128)} %get-tuple-element.26) | copy-start | bytes 12582916
  55.4 2.0 %copy-start.1 = (f32[32,8,512]{2,1,0:T(8,128)S(1)}, f32[32,8,512]{2,1,0:T(8,128)}, u32[]{:S(2)}) copy-start(f32[32,8,512]{2,1,0:T(8,128)} %get-tuple-element.15) | copy-start | bytes 1572868
  55.4 2.8 %copy-start.4 = (f32[1,512]{1,0:T(1,128)S(1)}, f32[1,512]{1,0:T(1,128)}, u32[]{:S(2)}) copy-start(f32[1,512]{1,0:T(1,128)} %get-tuple-element.16) | copy-start | bytes 6148
  55.4 3.4 %copy-start.2 = (f32[256,256]{1,0:T(8,128)S(1)}, f32[256,256]{1,0:T(8,128)}, u32[]{:S(2)}) copy-start(f32[256,256]{1,0:T(8,128)} %get-tuple-element.29) | copy-start | bytes 786436

commit v3 on v2

--- a/solution.py
+++ b/solution.py
@@ -25,7 +25,7 @@
 def step_kernel(groups, shards, slots, bags, tile, in_place, *refs):
     refs = list(refs)
     take = lambda n: [refs.pop(0) for _ in range(n)]
-    feats, t_in, t_out, table, weight, out_w, cols, rows = take(8)
+    feats, t_in, t_out, table, weight, out_w, ids, live, req_of, labels = take(10)
     scores, g_inter, g_out, g_table, tower_a, tower_b = take(6)
     pool_s, pool_r, feat_r, item_s, item_r, term_s, term_r = take(7)
     inter_s, inter_r, out_s, out_r, mine_s, users_r, part_s, part_r, sum_s, sum_r = take(10)
@@ -39,7 +39,7 @@
     rows_table, width = table.shape
     hidden_width = t_out.shape[0]
     units = weight.shape[1]
-    cands = cols.shape[0]
+    cands = shards * slots
     rows_user = feats.shape[0]
     group_rows = shards * rows_user
     sizes = {"all": total, "tbl": shards, "grp": groups, "far": total - shards + 1}
@@ -122,6 +122,21 @@
 
     lax.fori_loop(1, total, greet, 0)
 
+    slot = lax.broadcasted_iota(jnp.int32, (shards, slots), 1)
+    live_at = jnp.broadcast_to(live[...], (8, shards)).astype(F32).T[:, 0:1]
+    mask = jnp.where(slot.astype(F32) < live_at, 1.0, 0.0)
+    flat = lambda grid: jnp.concatenate([grid[d : d + 1] for d in range(shards)], axis=1)
+    rows = jnp.concatenate(
+        [
+            jnp.concatenate([ids[0, d].astype(F32) for d in range(shards)], axis=1),
+            flat(req_of[0].astype(F32)),
+            flat(mask),
+            flat(labels[0]),
+            jnp.zeros((-(bags + 3) % 8, cands), F32),
+        ],
+        axis=0,
+    )
+    cols = rows.T
     lane = lax.broadcasted_iota(jnp.int32, (cands, rows_table), 1).astype(F32)
     counts = jnp.zeros((cands, rows_table), F32)
     for bag in range(bags):
@@ -162,7 +177,9 @@
     sig = jax.nn.sigmoid(inner)
     act = inner * sig
     score = jnp.sum(act * out_w[...], axis=1, keepdims=True)
-    scores[...] = score
+    wide = jnp.broadcast_to(score, (cands, 128)).T
+    for d in range(shards):
+        scores[0, d : d + 1, :] = wide[0:1, d * slots : (d + 1) * slots]
     factor = 1.0 / math.sqrt(groups * shards * shards * slots)
     grad = cols[:, bags + 1 : bags + 2] * (jax.nn.sigmoid(score) - cols[:, bags + 2 : bags + 3]) * factor
     slope = sig * (1.0 + inner * (1.0 - sig))
@@ -215,10 +232,10 @@
 
         def behind(index, carry):
             at = pl.ds(pl.multiple_of(index * tile, tile), tile)
-            tower_b[at, :] = dot(hidden_t[at, :], d_users, 1, 0)
+            tower_b[at, :] = dot(hidden_t[at, :], d_users, 1, 0).astype(BF)
             d_hidden = dot(t_out[at, :], d_users_t, 1, 0)
             d_pre = (d_hidden * slope_t[at, :].astype(F32)).astype(BF)
-            tower_a[:, at] = dot(feats_t, d_pre, 1, 1)
+            tower_a[:, at] = dot(feats_t, d_pre, 1, 1).astype(BF)
             return carry
 
         lax.fori_loop(0, hidden_width // tile, behind, 0)
@@ -249,26 +266,15 @@
     tile = math.gcd(hidden_width, 512)
     in_place = rows_all <= 512
 
-    slot_index = jnp.arange(slots, dtype=jnp.int32)
-    mask = (slot_index[None, :] < live[0][:, None]).reshape(1, cands)
-    rows = jnp.concatenate(
-        [
-            jnp.swapaxes(ids[0], 0, 1).reshape(-1, cands).astype(F32),
-            req_of[0].reshape(1, cands).astype(F32),
-            mask.astype(F32),
-            labels[0].reshape(1, cands),
-            jnp.zeros((1, cands), F32),
-        ]
-    )
     struct = jax.ShapeDtypeStruct
     outs = [
-        struct((cands, 1), F32),
+        struct((1, shards, slots), F32),
         struct((total, width // total, units), F32),
         struct((1, units), F32),
         struct((rows_table, width), F32),
     ]
     if in_place:
-        outs += [struct(tower_in.shape, F32), struct(tower_out.shape, F32)]
+        outs += [struct(tower_in.shape, BF), struct(tower_out.shape, BF)]
     else:
         outs += [struct((total, rows_user, feats), BF), struct((total, rows_user, width), BF)]
     blocks = (shards, slots, width)
@@ -292,7 +298,7 @@
     score, inter_total, out_total, grad_table, first, second = pl.pallas_call(
         functools.partial(step_kernel, groups, shards, slots, ids.shape[2], tile, in_place),
         out_shape=outs,
-        in_specs=[vmem] * 8,
+        in_specs=[vmem] * 10,
         out_specs=[vmem] * 6,
         scratch_shapes=[pltpu.VMEM(shape, kind) for shape, kind in buffers]
         + [pltpu.SemaphoreType.DMA((10,))] * 3,
@@ -302,7 +308,7 @@
         name="ranking_step",
     )(
         user_feats, tower_in, tower_out, table, inter_weight,
-        out_weight.reshape(1, units), rows.T, rows,
+        out_weight.reshape(1, units), ids, live, req_of, labels,
     )
 
     def tower_grads(part_feats, part_users):
@@ -331,9 +337,9 @@
             (jnp.zeros(tower_in.shape, F32), jnp.zeros(tower_out.shape, F32)),
         )
     return (
-        score.reshape(1, shards, slots),
-        first,
-        second,
+        score,
+        first.astype(F32),
+        second.astype(F32),
         inter_total.reshape(width, units),
         out_total.reshape(units),
         grad_table,

time: 59.8 us -> 54 us (0.903)
  local copies, waits for them, and re-layouts: 9.88 us -> 2.69 us
  other arithmetic: 3.14 us -> 5.55 us
  Pallas kernels: 45.8 us -> 44.9 us
    unnamed x15 -> x14, local copies, waits for them, and re-layouts: 7.37 us -> 2.69 us
    convert_element_type x3 -> x2, other arithmetic: 2.14 us -> 5.55 us  [the longest x1 4.02 us: body(): second.astype(F32)]
    pallas_call x1 -> x0, other arithmetic: 1.01 us -> none  [body(): pl.pallas_call(functools.partial(step_kernel, groups, shards, slots, ids....]
    pallas_call x1, Pallas kernels: 45.8 us -> 44.9 us  [body(): pl.pallas_call(functools.partial(step_kernel, groups, shards, slots, ids....]
    transpose x1 -> x0, local copies, waits for them, and re-layouts: 0.79 us -> none  [body(): score, inter_total, out_total, grad_table, first, second = pl.pallas_call...]
    another operation x1 -> x0, local copies, waits for them, and re-layouts: 0.76 us -> none  [body(): labels[0].reshape(1, cands)]
    reshape x1 -> x0, local copies, waits for them, and re-layouts: 0.68 us -> none  [body(): score.reshape(1, shards, slots)]
where the time goes in v3:
time: 54 us; the launch traced here: 53.8 us
  Pallas kernels  44.9 us (83%)
  other arithmetic  5.55 us (10%)
  local copies, waits for them, and re-layouts  2.69 us (5%)
  between operations  0.67 us (1%)
    pallas_call x1, Pallas kernels, body(): pl.pallas_call(functools.partial(step_kernel, groups, shards, slots, ids....  44.9 us
    convert_element_type x1, other arithmetic, body(): second.astype(F32)  4.02 us
    unnamed x14, local copies, waits for them, and re-layouts  2.69 us
    convert_element_type x1, other arithmetic, body(): first.astype(F32)  1.53 us

profile of v3, /device:TPU:29, one launch (start us, length us, event | category | flops | bytes accessed | tf_op | source)
XLA Modules:
  0.0 53.8 jit_solution(5712570137557100899)
XLA Ops:
  0.6 44.9 %ranking_step.1 = (f32[1,8,32]{2,1,0:T(8,128)}, f32[32,8,512]{2,1,0:T(8,128)}, f32[1,512]{1,0:T(1,128)}, f32[256,256]{1,0:T(8,128)}, bf16[128,4096]{1,0:T(8,128)(2,1)}, /*index=5*/bf16[4096,256]{1,0:T(8,128)(2,1)}) custom-call(bf16[16,128]{1,0:T(8,128)(2,1)} %refs_0_.1, bf16[128,4096]{1,0:T(8,128)(2,1)} %refs_1_.1, bf16[4096,256]{1,0:T(8,128)(2,1)} %refs_2_.1, ...), custom_call_target="tpu_custom_call" | custom-call | tf_op jit(solution)/shard_map/ranking_step/pallas_call | solution.py:298
  45.6 0.0 copy-start
  45.6 4.0 %convert_element_type.7 = f32[4096,256]{1,0:T(8,128)} convert(bf16[4096,256]{1,0:T(8,128)(2,1)} %get-tuple-element.14) | non-fusion elementwise | flops 1048576 | bytes 6291456 | tf_op jit(solution)/shard_map/convert_element_type | solution.py:342
  49.6 0.0 copy-start.3
  49.6 0.0 copy-start.1
  49.6 0.0 copy-done
  49.6 0.0 copy-start.4
  49.6 0.0 copy-start.2
  49.6 1.5 %convert_element_type.6 = f32[128,4096]{1,0:T(8,128)} convert(bf16[128,4096]{1,0:T(8,128)(2,1)S(1)} %copy-done) | non-fusion elementwise | flops 524288 | bytes 3145728 | tf_op jit(solution)/shard_map/convert_element_type | solution.py:341
  51.1 0.0 copy-done.3
  51.1 0.6 %copy.20 = f32[1,8,32]{2,1,0:T(8,128)} copy(f32[1,8,32]{2,1,0:T(8,128)S(1)} %copy-done.3) | data formatting | bytes 2048
  51.7 0.0 copy-done.1
  51.7 0.8 %copy.21 = f32[256,512]{1,0:T(8,128)} copy(f32[256,512]{1,0:T(8,128)S(1)} %bitcast.3) | data formatting | bytes 1048576
  52.5 0.0 copy-done.4
  52.5 0.6 %copy.22 = f32[512]{0:T(512)} copy(f32[512]{0:T(512)S(1)} %bitcast.5) | data formatting | bytes 4096
  53.1 0.0 copy-done.2
  53.1 0.7 %copy.23 = f32[256,256]{1,0:T(8,128)} copy(f32[256,256]{1,0:T(8,128)S(1)} %copy-done.2) | data formatting | bytes 524288
Async XLA Ops:
  45.6 4.0 %copy-start = (bf16[128,4096]{1,0:T(8,128)(2,1)S(1)}, bf16[128,4096]{1,0:T(8,128)(2,1)}, u32[]{:S(2)}) copy-start(bf16[128,4096]{1,0:T(8,128)(2,1)} %get-tuple-element.13) | copy-start | bytes 3145732
  49.6 1.6 %copy-start.3 = (f32[1,8,32]{2,1,0:T(8,128)S(1)}, f32[1,8,32]{2,1,0:T(8,128)}, u32[]{:S(2)}) copy-start(f32[1,8,32]{2,1,0:T(8,128)} %get-tuple-element.24) | copy-start | bytes 3076
  49.6 2.1 %copy-start.1 = (f32[32,8,512]{2,1,0:T(8,128)S(1)}, f32[32,8,512]{2,1,0:T(8,128)}, u32[]{:S(2)}) copy-start(f32[32,8,512]{2,1,0:T(8,128)} %get-tuple-element.15) | copy-start | bytes 1572868
  49.6 2.9 %copy-start.4 = (f32[1,512]{1,0:T(1,128)S(1)}, f32[1,512]{1,0:T(1,128)}, u32[]{:S(2)}) copy-start(f32[1,512]{1,0:T(1,128)} %get-tuple-element.16) | copy-start | bytes 6148
  49.6 3.5 %copy-start.2 = (f32[256,256]{1,0:T(8,128)S(1)}, f32[256,256]{1,0:T(8,128)}, u32[]{:S(2)}) copy-start(f32[256,256]{1,0:T(8,128)} %get-tuple-element.29) | copy-start | bytes 786436

commit v4 on v3

--- a/solution.py
+++ b/solution.py
@@ -28,6 +28,7 @@
     feats, t_in, t_out, table, weight, out_w, ids, live, req_of, labels = take(10)
     scores, g_inter, g_out, g_table, tower_a, tower_b = take(6)
     pool_s, pool_r, feat_r, item_s, item_r, term_s, term_r = take(7)
+    half_s, half_r = take(2)
     inter_s, inter_r, out_s, out_r, mine_s, users_r, part_s, part_r, sum_s, sum_r = take(10)
     if in_place:
         t_in_t, hidden_t, slope_t = take(3)
@@ -36,29 +37,38 @@
     my_grp = lax.axis_index("grp")
     my_tbl = lax.axis_index("tbl")
     me = my_grp * shards + my_tbl
+    half = total // 2
+    core = my_grp % 2
+    chip = (my_grp // 2) * shards + my_tbl
+    slot_of_me = core * half + chip
     rows_table, width = table.shape
     hidden_width = t_out.shape[0]
     units = weight.shape[1]
     cands = shards * slots
     rows_user = feats.shape[0]
     group_rows = shards * rows_user
-    sizes = {"all": total, "tbl": shards, "grp": groups, "far": total - shards + 1}
-    places = {"all": me, "tbl": my_tbl, "grp": my_grp}
+    sizes = {"all": total, "tbl": shards, "grp": groups, "far": total - shards + 1, "chip": half, "pair": 2}
+    places = {"all": me, "tbl": my_tbl, "grp": my_grp, "chip": chip, "pair": core}
     links = {
         "pool": (0, "tbl", pool_s, pool_r, True),
         "near": (1, "tbl", feats, feat_r, False),
         "far": (2, "far", feats, feat_r, False),
         "item": (3, "tbl", item_s, item_r, True),
         "term": (4, "tbl", term_s, term_r, True),
-        "inter": (5, "all", inter_s, inter_r, True),
+        "halves": (10, "pair", half_s, half_r, True),
+        "inter": (5, "chip", inter_s, inter_r, True),
         "out": (6, "all", out_s, out_r, False),
-        "mine": (7, "all", mine_s, users_r, False),
+        "mine": (7, "chip", mine_s, users_r.at[core], False),
+        "twin": (11, "pair", users_r.at[core], users_r, False),
         "part": (8, "grp", part_s, part_r, False),
-        "sum": (9, "all", sum_s, sum_r, False),
+        "sum": (9, "chip", sum_s, sum_r.at[core], False),
+        "join": (12, "pair", sum_r.at[core], sum_r, False),
     }
 
+    alone = ("far", "twin", "join")
+
     def spot(name):
-        return me if name in ("near", "far") else places[links[name][1]]
+        return slot_of_me if name in ("near", "far") else places[links[name][1]]
 
     def origin(name, where):
         _, _, source, _, scatter = links[name]
@@ -72,7 +82,7 @@
     def push(*names):
         scope = links[names[0]][1]
         for name in names:
-            if name != "far":
+            if name not in alone:
                 own(name).start()
 
         def one(step, carry):
@@ -82,6 +92,12 @@
             elif scope == "tbl":
                 there = lax.rem(my_tbl + step, shards)
                 device = (my_grp, there)
+            elif scope == "chip":
+                there = lax.rem(chip + step, half)
+                device = ((there // shards) * 2 + core, there % shards)
+            elif scope == "pair":
+                there = 1 - core
+                device = (my_grp + 1 - 2 * core, my_tbl)
             elif scope == "grp":
                 there = lax.rem(my_grp + step, groups)
                 device = (there, my_tbl)
@@ -107,7 +123,7 @@
         return target.at[pl.ds(0, sizes[scope] - 1)]
 
     def arrive(name):
-        if name != "far":
+        if name not in alone:
             own(name).wait()
         pltpu.make_async_copy(others(name), others(name), recv_sem.at[links[name][0]]).wait()
 
@@ -156,7 +172,7 @@
         lax.fori_loop(0, hidden_width // tile, flip, 0)
 
     arrive("near")
-    group_feats = feat_r[pl.ds(my_grp * shards, shards)].reshape(group_rows, -1)
+    group_feats = feat_r[pl.ds(core * half + (my_grp // 2) * shards, shards)].reshape(group_rows, -1)
 
     def forward(index, acc):
         at = pl.ds(pl.multiple_of(index * tile, tile), tile)
@@ -193,8 +209,9 @@
     push("term", "item")
     out_s[...] = jnp.sum(grad * act, axis=0, keepdims=True)
     inter = dot(cross, dinner, 0, 0)
-    inter_s[...] = inter.reshape(total, width // total, units).astype(BF)
-    push("inter", "out")
+    half_s[...] = inter.reshape(2, width // 2, units).astype(BF)
+    push("halves")
+    push("out")
     arrive("far")
     all_rows = total * rows_user
     if in_place:
@@ -212,6 +229,10 @@
     arrive("term")
     mine_s[...] = jnp.sum(term_r[...].astype(F32), axis=0).astype(BF)
     push("mine")
+    arrive("halves")
+    paired = jnp.sum(half_r[...].astype(F32), axis=0)
+    inter_s[...] = paired.reshape(half, width // total, units).astype(BF)
+    push("inter")
     arrive("item")
     side = lax.broadcasted_iota(jnp.int32, (rows_table, cands), 0).astype(F32)
     counts_t = jnp.zeros((rows_table, cands), F32)
@@ -219,12 +240,14 @@
         counts_t = counts_t + jnp.where(rows[bag : bag + 1, :] == side, 1.0, 0.0)
     part_s[...] = dot(counts_t.astype(BF), item_r[...].reshape(cands, width), 1, 0).astype(BF)
     push("part")
+    arrive("mine")
+    push("twin")
     arrive("inter")
     sum_s[...] = jnp.sum(inter_r[...].astype(F32), axis=0).astype(BF)
     push("sum")
     arrive("out")
     g_out[...] = jnp.sum(out_r[...], axis=0)
-    arrive("mine")
+    arrive("twin")
     if in_place:
         d_users = users_r[...].reshape(all_rows, width)
         d_users_t = d_users.T
@@ -238,14 +261,20 @@
             tower_a[:, at] = dot(feats_t, d_pre, 1, 1).astype(BF)
             return carry
 
-        lax.fori_loop(0, hidden_width // tile, behind, 0)
+        middle = hidden_width // tile // 2
+        lax.fori_loop(0, middle, behind, 0)
+        arrive("sum")
+        push("join")
+        lax.fori_loop(middle, hidden_width // tile, behind, 0)
     else:
+        arrive("sum")
+        push("join")
         tower_a[...] = feat_r[...]
-        tower_b[...] = users_r[...]
+        tower_b[...] = users_r[...].reshape(tower_b.shape)
     arrive("part")
     g_table[...] = jnp.sum(part_r[...].astype(F32), axis=0)
-    arrive("sum")
-    g_inter[...] = sum_r[...].astype(F32)
+    arrive("join")
+    g_inter[...] = sum_r[...].reshape(g_inter.shape).astype(F32)
     for name in links:
         pltpu.make_async_copy(others(name), others(name), send_sem.at[links[name][0]]).wait()
 
@@ -279,14 +308,16 @@
         outs += [struct((total, rows_user, feats), BF), struct((total, rows_user, width), BF)]
     blocks = (shards, slots, width)
     terms = (shards, rows_user, width)
-    inter = (total, width // total, units)
+    inter = (total // 2, width // total, units)
+    halves = (2, width // 2, units)
+    twins = (2, total // 2, rows_user, width)
     buffers = [
         (blocks, BF), (blocks, BF), ((total, rows_user, feats), BF),
         (blocks, BF), (blocks, BF), (terms, BF), (terms, BF),
-        (inter, BF), (inter, BF), ((1, units), F32), ((total, 1, units), F32),
-        ((rows_user, width), BF), ((total, rows_user, width), BF),
+        (halves, BF), (halves, BF), (inter, BF), (inter, BF), ((1, units), F32), ((total, 1, units), F32),
+        ((rows_user, width), BF), (twins, BF),
         ((rows_table, width), BF), ((groups, rows_table, width), BF),
-        (inter[1:], BF), (inter, BF),
+        (inter[1:], BF), ((2,) + inter, BF),
     ]
     if in_place:
         buffers += [
@@ -301,7 +332,7 @@
         in_specs=[vmem] * 10,
         out_specs=[vmem] * 6,
         scratch_shapes=[pltpu.VMEM(shape, kind) for shape, kind in buffers]
-        + [pltpu.SemaphoreType.DMA((10,))] * 3,
+        + [pltpu.SemaphoreType.DMA((13,))] * 3,
         compiler_params=pltpu.CompilerParams(
             collective_id=0, has_side_effects=True, vmem_limit_bytes=60 * 1024 * 1024
         ),

time: 54 us -> 50.6 us (0.937)
  the two profiles are of different devices: /device:TPU:29 before, /device:TPU:0 now
where the time goes in v4:
time: 50.6 us; the launch traced here: 50.4 us
  Pallas kernels  41.5 us (82%)
  other arithmetic  5.55 us (11%)
  local copies, waits for them, and re-layouts  2.69 us (5%)
  between operations  0.67 us (1%)
    pallas_call x1, Pallas kernels, body(): pl.pallas_call(functools.partial(step_kernel, groups, shards, slots, ids....  41.5 us
    convert_element_type x1, other arithmetic, body(): second.astype(F32)  4.02 us
    unnamed x14, local copies, waits for them, and re-layouts  2.69 us
    convert_element_type x1, other arithmetic, body(): first.astype(F32)  1.53 us

profile of v4, /device:TPU:0, one launch (start us, length us, event | category | flops | bytes accessed | tf_op | source)
XLA Modules:
  0.0 50.4 jit_solution(17621758274782885379)
XLA Ops:
  0.6 41.5 %ranking_step.1 = (f32[1,8,32]{2,1,0:T(8,128)}, f32[32,8,512]{2,1,0:T(8,128)}, f32[1,512]{1,0:T(1,128)}, f32[256,256]{1,0:T(8,128)}, bf16[128,4096]{1,0:T(8,128)(2,1)}, /*index=5*/bf16[4096,256]{1,0:T(8,128)(2,1)}) custom-call(bf16[16,128]{1,0:T(8,128)(2,1)} %refs_0_.1, bf16[128,4096]{1,0:T(8,128)(2,1)} %refs_1_.1, bf16[4096,256]{1,0:T(8,128)(2,1)} %refs_2_.1, ...), custom_call_target="tpu_custom_call" | custom-call | tf_op jit(solution)/shard_map/ranking_step/pallas_call | solution.py:329
  42.2 0.0 copy-start
  42.2 4.0 %convert_element_type.7 = f32[4096,256]{1,0:T(8,128)} convert(bf16[4096,256]{1,0:T(8,128)(2,1)} %get-tuple-element.14) | non-fusion elementwise | flops 1048576 | bytes 6291456 | tf_op jit(solution)/shard_map/convert_element_type | solution.py:373
  46.2 0.0 copy-start.3
  46.2 0.0 copy-start.1
  46.2 0.0 copy-done
  46.2 0.0 copy-start.4
  46.2 0.0 copy-start.2
  46.2 1.5 %convert_element_type.6 = f32[128,4096]{1,0:T(8,128)} convert(bf16[128,4096]{1,0:T(8,128)(2,1)S(1)} %copy-done) | non-fusion elementwise | flops 524288 | bytes 3145728 | tf_op jit(solution)/shard_map/convert_element_type | solution.py:372
  47.8 0.0 copy-done.3
  47.8 0.6 %copy.20 = f32[1,8,32]{2,1,0:T(8,128)} copy(f32[1,8,32]{2,1,0:T(8,128)S(1)} %copy-done.3) | data formatting | bytes 2048
  48.4 0.0 copy-done.1
  48.4 0.8 %copy.21 = f32[256,512]{1,0:T(8,128)} copy(f32[256,512]{1,0:T(8,128)S(1)} %bitcast.3) | data formatting | bytes 1048576
  49.2 0.0 copy-done.4
  49.2 0.6 %copy.22 = f32[512]{0:T(512)} copy(f32[512]{0:T(512)S(1)} %bitcast.5) | data formatting | bytes 4096
  49.7 0.0 copy-done.2
  49.7 0.7 %copy.23 = f32[256,256]{1,0:T(8,128)} copy(f32[256,256]{1,0:T(8,128)S(1)} %copy-done.2) | data formatting | bytes 524288
Async XLA Ops:
  42.2 4.0 %copy-start = (bf16[128,4096]{1,0:T(8,128)(2,1)S(1)}, bf16[128,4096]{1,0:T(8,128)(2,1)}, u32[]{:S(2)}) copy-start(bf16[128,4096]{1,0:T(8,128)(2,1)} %get-tuple-element.13) | copy-start | bytes 3145732
  46.2 1.6 %copy-start.3 = (f32[1,8,32]{2,1,0:T(8,128)S(1)}, f32[1,8,32]{2,1,0:T(8,128)}, u32[]{:S(2)}) copy-start(f32[1,8,32]{2,1,0:T(8,128)} %get-tuple-element.24) | copy-start | bytes 3076
  46.2 2.1 %copy-start.1 = (f32[32,8,512]{2,1,0:T(8,128)S(1)}, f32[32,8,512]{2,1,0:T(8,128)}, u32[]{:S(2)}) copy-start(f32[32,8,512]{2,1,0:T(8,128)} %get-tuple-element.15) | copy-start | bytes 1572868
  46.2 2.9 %copy-start.4 = (f32[1,512]{1,0:T(1,128)S(1)}, f32[1,512]{1,0:T(1,128)}, u32[]{:S(2)}) copy-start(f32[1,512]{1,0:T(1,128)} %get-tuple-element.16) | copy-start | bytes 6148
  46.2 3.5 %copy-start.2 = (f32[256,256]{1,0:T(8,128)S(1)}, f32[256,256]{1,0:T(8,128)}, u32[]{:S(2)}) copy-start(f32[256,256]{1,0:T(8,128)} %get-tuple-element.29) | copy-start | bytes 786436
